TPU v7x, 32 devices: a whole 2x2x4 slice. The times are simulated.
32 devices in a mesh: row: 4 (over x, core), col: 8 (over z, y).
Axes of the slice: x: 2, y: 2, z: 4, core: 2. Of those that a mesh axis runs over, the one named last changes fastest.
Arguments:
- corner: bfloat16 [25600, 25600], P('row', 'col'), may hold values from -32 to 32
- edge: bfloat16 [25600, 25600], P('row', 'col'), may hold values from -32 to 32
- sketch: bfloat16 [25600, 448], P('col'), may hold values from -6 to 6
Outputs:
- corner_new: float32 [400, 400], replicated
- edge_new: float32 [400, 400], replicated
All inputs are finite; a program needn't handle non-finite values.
Results may differ from a plain program's by a relative error of at most 0.0015.
Values may be sent and summed in bfloat16 or wider, within the bound.
A program may use at most 256 MiB of HBM per device.

v0:
```python
import jax
import jax.numpy as jnp
from jax import lax
from jax.sharding import PartitionSpec as P

RANK = 400


def from_root(value, axis, source):
    kept = jnp.where(lax.axis_index(axis) == source, value, 0).astype(value.dtype)
    return lax.psum(kept, axis)


def project(sampled, gram):
    lower = jnp.linalg.cholesky(gram)
    basis = lax.linalg.triangular_solve(
        lower, sampled, left_side=False, lower=True, transpose_a=True
    )
    return basis[:, basis.shape[1] - RANK :].astype(jnp.bfloat16)


def gram_of(sampled):
    return jnp.dot(sampled.T, sampled, precision=lax.Precision.HIGHEST)


def exact_left(narrow_rows, image):
    upper_part = image.astype(jnp.bfloat16)
    lower_part = (image - upper_part.astype(jnp.float32)).astype(jnp.bfloat16)
    first = jnp.dot(narrow_rows.T, upper_part, preferred_element_type=jnp.float32)
    second = jnp.dot(narrow_rows.T, lower_part, preferred_element_type=jnp.float32)
    return first + second


def body(corner, edge, sketch):
    partial_sample = jnp.dot(corner, sketch, preferred_element_type=jnp.float32)
    sampled = lax.psum(partial_sample, "col")
    gram = lax.psum(gram_of(sampled), "row")
    rows_proj = project(sampled, gram)
    width = corner.shape[1]
    ratio = lax.axis_size("col") // lax.axis_size("row")
    col_index = lax.axis_index("col")
    offered = lax.dynamic_slice_in_dim(rows_proj, col_index % ratio * width, width, 0)
    cols_proj = from_root(offered, "row", col_index // ratio)
    corner_part = jnp.dot(corner, cols_proj, preferred_element_type=jnp.float32)
    edge_part = jnp.dot(edge, cols_proj, preferred_element_type=jnp.float32)
    corner_image, edge_image = lax.psum((corner_part, edge_part), "col")
    corner_local = exact_left(rows_proj, corner_image)
    edge_local = exact_left(rows_proj, edge_image)
    corner_new, edge_new = lax.psum((corner_local, edge_local), "row")
    return (corner_new, edge_new)


def solution(mesh):
    placed = (P("row", "col"), P("row", "col"), P("col", None))
    return jax.shard_map(body, mesh=mesh, in_specs=placed, out_specs=(P(), P()), check_vma=False)
```

profile of v0, /device:TPU:0, one launch (start us, length us, event | category | flops | bytes accessed | tf_op | source)
XLA Modules:
  0.0 1422.3 jit_solution(11598771712403457499)
XLA Ops:
  9.0 28.2 %fusion.52 = f32[6400,448]{0,1:T(8,128)} fusion(bf16[6400,3200]{1,0:T(8,128)(2,1)} %param.3, bf16[3200,448]{0,1:T(8,128)(2,1)S(1)} %copy-done), kind=kOutput, calls=%fused_computation.95 | convolution fusion | flops 18350080000 | bytes 55296000 | tf_op jit(solution)/shard_map/dot_general | solution.py:35
  37.3 356.6 %all-reduce.11.cloned.1.call-done = f32[6400,448]{0,1:T(8,128)} async-done(((f32[6400,448]{0,1:T(8,128)}), f32[6400,448]{0,1:T(8,128)}) %all-reduce.11.cloned.1.call-update) | async-done | bytes 11468816 | tf_op jit(solution)/shard_map/psum | solution.py:36
  393.9 22.2 %fusion.53 = f32[448,448]{0,1:T(8,128)} fusion(f32[6400,448]{0,1:T(8,128)} %all-reduce.11.cloned.1.call-done), kind=kOutput, calls=%fused_computation.96 | convolution fusion | flops 15414067200 | bytes 12271616 | tf_op jit(solution)/shard_map/dot_general | solution.py:23
  416.8 34.3 %all-reduce.13.cloned.1.call-done = f32[448,448]{0,1:T(8,128)} async-done(((f32[448,448]{0,1:T(8,128)}), f32[448,448]{0,1:T(8,128)}) %all-reduce.13.cloned.1.call-update) | async-done | bytes 802832 | tf_op jit(solution)/shard_map/psum | solution.py:37
  454.0 11.7 cholesky.105
  465.7 9.8 custom-call.30
  476.3 11.7 cholesky.219
  488.0 9.9 custom-call.31
  498.6 11.7 cholesky.240
  511.0 9.8 custom-call.32
  521.3 5.8 cholesky.260
  531.1 6.0 while.1
  537.3 39.5 %custom-call.33 = f32[4,128,128]{1,2,0:T(8,128)S(1)} custom-call(f32[4,128,128]{2,1,0:T(8,128)S(1)} %pad_maximum_fusion.3), custom_call_target="InvertDiagBlocksLowerTriangular" | custom-call | tf_op jit(solution)/shard_map/triangular_solve | solution.py:16
  576.8 5.1 fusion.51
  581.9 5.3 convolution_subtract_fusion.1
  587.2 3.2 fusion.50
  590.4 6.7 convolution_subtract_fusion
  597.1 3.2 fusion.49
  600.3 7.4 fusion.6
  610.2 2.2 copy-done.2
  612.5 1.9 dynamic-slice_select_fusion
  614.5 59.5 %all-reduce.15.cloned.1.call-done = bf16[3200,400]{0,1:T(8,128)(2,1)} async-done(((bf16[3200,400]{0,1:T(8,128)(2,1)}), bf16[3200,400]{0,1:T(8,128)(2,1)}) %all-reduce.15.cloned.1.call-update) | async-done | bytes 2560016 | tf_op jit(solution)/shard_map/psum | solution.py:11
  674.0 29.0 %convolution_bitcast_fusion.1 = f32[6400,400]{0,1:T(8,128)} fusion(bf16[3200,400]{0,1:T(8,128)(2,1)} %all-reduce.15.cloned.1.call-done, bf16[6400,3200]{1,0:T(8,128)(2,1)} %param.3), kind=kOutput, calls=%fused_computation.3 | convolution fusion | flops 16384000000 | bytes 53760000 | tf_op jit(solution)/shard_map/dot_general | solution.py:44
  703.0 25.5 %convolution_bitcast_fusion = f32[6400,400]{0,1:T(8,128)} fusion(bf16[3200,400]{0,1:T(8,128)(2,1)S(1)} %copy-done.4, bf16[6400,3200]{1,0:T(8,128)(2,1)} %param.4), kind=kOutput, calls=%fused_computation.2 | convolution fusion | flops 16384000000 | bytes 53760000 | tf_op jit(solution)/shard_map/dot_general | solution.py:45
  728.6 613.7 %all-reduce.17.cloned.1.call-done = (f32[6400,400]{0,1:T(8,128)}, f32[6400,400]{0,1:T(8,128)}) async-done(((f32[6400,400]{0,1:T(8,128)}, f32[6400,400]{0,1:T(8,128)}), (f32[6400,400]{0,1:T(8,128)}, f32[6400,400]{0,1:T(8,128)})) %all-reduce.17.cloned.1.call-update) | async-done | bytes 20480016 | tf_op jit(solution)/shard_map/psum | solution.py:46
  1342.3 12.1 fusion.12
  1354.4 7.1 fusion.22
  1361.5 2.8 fusion.13
  1364.4 3.7 fusion.25
  1368.1 43.2 %all-reduce.19.cloned.1.call-done = (f32[400,400]{1,0:T(8,128)}, f32[400,400]{1,0:T(8,128)}) async-done(((f32[400,400]{1,0:T(8,128)}, f32[400,400]{1,0:T(8,128)}), (f32[400,400]{1,0:T(8,128)}, f32[400,400]{1,0:T(8,128)})) %all-reduce.19.cloned.1.call-update) | async-done | bytes 1280016 | tf_op jit(solution)/shard_map/psum | solution.py:49
  1411.3 2.1 copy.29
  1413.4 2.1 copy.30
  (70 shorter events, 18.0 us)
Async XLA Ops:
  7.2 1.8 copy-start
  7.2 386.7 %all-reduce.11.cloned.1.call-start = ((), (), s32[]{:S(2)}) async-start(), calls=%async_computation | async-start | bytes 22937600 | tf_op jit(solution)/shard_map/psum | solution.py:36
  37.2 413.8 %all-reduce.13.cloned.1.call-start = ((), (), s32[]{:S(2)}) async-start(), calls=%async_computation.1 | async-start | bytes 1835008 | tf_op jit(solution)/shard_map/psum | solution.py:37
  416.1 257.9 %all-reduce.15.cloned.1.call-start = ((), (), s32[]{:S(2)}) async-start(), calls=%async_computation.2 | async-start | bytes 5120000 | tf_op jit(solution)/shard_map/psum | solution.py:11
  610.2 2.2 copy-start.2
  614.4 727.9 %all-reduce.17.cloned.1.call-start = ((), (), s32[]{:S(2)}) async-start(), calls=%async_computation.3 | async-start | bytes 40960000 | tf_op jit(solution)/shard_map/psum | solution.py:46
  674.0 29.0 %copy-start.4 = (bf16[3200,400]{0,1:T(8,128)(2,1)S(1)}, bf16[3200,400]{0,1:T(8,128)(2,1)}, u32[]{:S(2)}) copy-start(bf16[3200,400]{0,1:T(8,128)(2,1)} %all-reduce.15.cloned.1.call-done) | copy-start | bytes 7680004
  728.5 682.8 %all-reduce.19.cloned.1.call-start = ((), (), s32[]{:S(2)}) async-start(), calls=%async_computation.4 | async-start | bytes 3276800 | tf_op jit(solution)/shard_map/psum | solution.py:49
  1342.3 12.1 copy-start.3
  1342.3 19.2 %slice-start = ((s8[5120000]{0:T(1024)(128)(4,1)}), s8[4194304]{0:T(1024)(128)(4,1)S(1)}, s32[]{:S(2)}) async-start(s8[5120000]{0:T(1024)(128)(4,1)} %bitcast.72), calls=%async_computation.5 | async-start | bytes 8388608
  1342.3 19.2 %slice-start.2 = ((s8[10240000]{0:T(1024)(128)(4,1)}), s8[4194304]{0:T(1024)(128)(4,1)S(1)}, s32[]{:S(2)}) async-start(s8[10240000]{0:T(1024)(128)(4,1)} %bitcast.74), calls=%async_computation.7 | async-start | bytes 8388608
  1342.3 19.2 %slice-start.3 = ((s8[10240000]{0:T(1024)(128)(4,1)}), s8[4194304]{0:T(1024)(128)(4,1)S(1)}, s32[]{:S(2)}) async-start(s8[10240000]{0:T(1024)(128)(4,1)} %bitcast.74), calls=%async_computation.8 | async-start | bytes 8388608
  1354.4 7.1 slice-start.1
  1354.4 7.1 slice-start.4
  1364.4 51.1 %copy-start.1 = (bf16[3200,448]{0,1:T(8,128)(2,1)S(1)}, bf16[3200,448]{0,1:T(8,128)(2,1)}, u32[]{:S(2)}) copy-start(bf16[3200,448]{0,1:T(8,128)(2,1)} %param.5) | copy-start | bytes 8601604
Sparse Core Ops, SparseCore 0:
  37.4 356.4 all-reduce.10
  416.2 34.8 all-reduce.12
  614.5 59.3 all-reduce.14
  728.7 613.5 all-reduce.16
  1368.3 43.0 all-reduce.18
where the time goes:
time: 1430 us; the launch traced here: 1420 us
  waiting for transfers between devices  1110 us (78%)
  matrix products  165 us (12%)
  other arithmetic  117 us (8%)
  between operations  17 us (1%)
  local copies, waits for them, and re-layouts  15.8 us (1%)
    psum x1, waiting for transfers between devices, body(): corner_image, edge_image = lax.psum((corner_part, edge_part), 'col')  614 us
    psum x1, waiting for transfers between devices, body(): sampled = lax.psum(partial_sample, 'col')  357 us
    another operation x14, other arithmetic, project(): lower = jnp.linalg.cholesky(gram)  72.7 us
    psum x1, waiting for transfers between devices, from_root(): return lax.psum(kept, axis)  59.5 us
    psum x1, waiting for transfers between devices, body(): corner_new, edge_new = lax.psum((corner_local, edge_local), 'row')  43.2 us
    another operation x8, other arithmetic, project(): lax.linalg.triangular_solve(lower, sampled, left_side=False, lower=True,...  40.7 us
    psum x1, waiting for transfers between devices, body(): gram = lax.psum(gram_of(sampled), 'row')  34.3 us
    another operation x7, matrix products, project(): lax.linalg.triangular_solve(lower, sampled, left_side=False, lower=True,...  32.4 us
  transfers between devices with their start and end apart: 5, of which 5 were waited for; matrix products, arithmetic and copies ran while one was open for 0% of the time, Pallas kernels for 0%

commit v1 on v0

v1 whole, which is shorter than its diff:
```python
import jax
import jax.numpy as jnp
from jax import lax
from jax.sharding import PartitionSpec as P

RANK = 400
HIGHEST = lax.Precision.HIGHEST


def outer(left, right):
    return lax.dot_general(left, right, (((0,), (0,)), ((), ())), preferred_element_type=jnp.float32)


def exact_left(rows, image):
    upper_part = image.astype(jnp.bfloat16)
    lower_part = (image - upper_part.astype(jnp.float32)).astype(jnp.bfloat16)
    return outer(rows, upper_part) + outer(rows, lower_part)


def inverse_factor(gram):
    lower = jnp.linalg.cholesky(gram)
    unit = jnp.eye(gram.shape[0], dtype=gram.dtype)
    inverse = lax.linalg.triangular_solve(lower, unit, left_side=True, lower=True)
    return inverse[gram.shape[0] - RANK :]


def column_route(n_row, n_col):
    ratio = n_col // n_row
    route = []
    for source in range(n_row):
        for shard in range(n_col):
            half, target = divmod(shard, n_row)
            route.append((source * n_col + shard, target * n_col + source * ratio + half))
    return route


def body(corner, edge, sketch):
    n_row, n_col = lax.axis_size("row"), lax.axis_size("col")
    both = ("row", "col")
    part = jnp.dot(corner, sketch, preferred_element_type=jnp.float32).astype(jnp.bfloat16)
    shard = lax.psum_scatter(part, "col", scatter_dimension=0, tiled=True)
    gram = lax.psum(outer(shard, shard), both)
    moved = lax.ppermute(shard, both, column_route(n_row, n_col))
    cols = lax.all_gather(moved, "row", axis=0, tiled=True)
    rows = lax.all_gather(shard, "col", axis=0, tiled=True)
    inverse = inverse_factor(gram)

    def renormalize(matrix):
        image = jnp.dot(matrix, cols, preferred_element_type=jnp.float32)
        total = exact_left(rows, image)
        half = jnp.dot(inverse, total, precision=HIGHEST)
        return lax.dot_general(half, inverse, (((1,), (1,)), ((), ())), precision=HIGHEST)

    return lax.psum((renormalize(corner), renormalize(edge)), both)


def solution(mesh):
    placed = (P("row", "col"), P("row", "col"), P("col", None))
    return jax.shard_map(body, mesh=mesh, in_specs=placed, out_specs=(P(), P()), check_vma=False)
```

time: 1430 us -> 726 us (0.51)
  waiting for transfers between devices: 1110 us -> 394 us
  local copies, waits for them, and re-layouts: 15.8 us -> 62.8 us
  matrix products: 165 us -> 131 us
    psum x5 -> x2, waiting for transfers between devices: 1110 us -> 269 us  [the longest x1 137 us: body(): gram = lax.psum(outer(shard, shard), both)]
    unnamed x5 -> x6, waiting for transfers between devices: 0.08 us -> 125 us
    unnamed x22 -> x30, local copies, waits for them, and re-layouts: 8.21 us -> 37.1 us
    another operation x13, matrix products: 34 us -> 10.5 us  [the longest x7 5.47 us: inverse_factor(): lax.linalg.triangular_solve(lower, unit, left_side=True, lower=True)]
    all_gather x0 -> x2, local copies, waits for them, and re-layouts: none -> 15.3 us  [the longest x1 9.16 us: body(): rows = lax.all_gather(shard, 'col', axis=0, tiled=True)]
    dot_general x8 -> x12, matrix products: 131 us -> 120 us  [the longest x2 57.5 us: renormalize(): image = jnp.dot(matrix, cols, preferred_element_type=jnp.float32)]
    another operation x22 -> x21, other arithmetic: 113 us -> 112 us  [the longest x14 72.9 us: inverse_factor(): lower = jnp.linalg.cholesky(gram)]
  transfers between devices with their start and end apart: 5 -> 6, of which waited for: 5 -> 3; matrix products, arithmetic and copies ran while one was open for 0% -> 29% of each run, Pallas kernels for 0% -> 0%
where the time goes in v1:
time: 726 us; the launch traced here: 720 us
  waiting for transfers between devices  394 us (54%)
  matrix products  131 us (18%)
  other arithmetic  114 us (16%)
  local copies, waits for them, and re-layouts  62.8 us (9%)
  between operations  17.2 us (2%)
    psum x1, waiting for transfers between devices, body(): gram = lax.psum(outer(shard, shard), both)  137 us
    psum x1, waiting for transfers between devices, body(): return lax.psum((renormalize(corner), renormalize(edge)), both)  132 us
    unnamed x6, waiting for transfers between devices  125 us
    another operation x14, other arithmetic, inverse_factor(): lower = jnp.linalg.cholesky(gram)  72.9 us
    dot_general x2, matrix products, renormalize(): image = jnp.dot(matrix, cols, preferred_element_type=jnp.float32)  57.5 us
    another operation x7, other arithmetic, inverse_factor(): lax.linalg.triangular_solve(lower, unit, left_side=True, lower=True)  39.5 us
    unnamed x30, local copies, waits for them, and re-layouts  37.1 us
    dot_general x1, matrix products, body(): jnp.dot(corner, sketch, preferred_element_type=jnp.float32)  27.6 us
  transfers between devices with their start and end apart: 6, of which 3 were waited for; matrix products, arithmetic and copies ran while one was open for 29% of the time, Pallas kernels for 0%

profile of v1, /device:TPU:0, one launch (start us, length us, event | category | flops | bytes accessed | tf_op | source)
XLA Modules:
  0.0 720.3 jit_solution(4127353241187174518)
XLA Ops:
  9.0 27.6 %convolution_convert_fusion = bf16[6400,448]{0,1:T(8,128)(2,1)} fusion(bf16[6400,3200]{1,0:T(8,128)(2,1)} %param.3, bf16[3200,448]{0,1:T(8,128)(2,1)S(1)} %copy-done), kind=kOutput, calls=%fused_computation.8 | convolution fusion | flops 18352947200 | bytes 49561600 | tf_op jit(solution)/shard_map/dot_general | solution.py:40
  36.5 9.2 %copy.22 = bf16[6400,448]{1,0:T(8,128)(2,1)} copy(bf16[6400,448]{0,1:T(8,128)(2,1)} %convolution_convert_fusion) | data formatting | bytes 11468800
  45.9 124.6 %reduce-scatter.4.cloned.1.call-done = bf16[800,448]{1,0:T(8,128)(2,1)} async-done(((bf16[6400,448]{1,0:T(8,128)(2,1)}), bf16[800,448]{1,0:T(8,128)(2,1)}) %reduce-scatter.4.cloned.1.call-update) | async-done | bytes 716816
  172.9 3.1 fusion.59
  177.9 137.3 %all-reduce.7.cloned.1.call-done = f32[448,448]{0,1:T(8,128)} async-done(((f32[448,448]{0,1:T(8,128)}), f32[448,448]{0,1:T(8,128)}) %all-reduce.7.cloned.1.call-update) | async-done | bytes 802832 | tf_op jit(solution)/shard_map/psum | solution.py:42
  319.0 11.7 %cholesky.105 = f32[128,128]{1,0:T(8,128)S(1)} custom-call(f32[128,128]{1,0:T(8,128)S(1)} %cholesky.272), custom_call_target="Cholesky" | custom-call | tf_op jit(solution)/shard_map/jit(cholesky)/cholesky | solution.py:21
  330.8 9.8 %custom-call.30 = f32[1,128,128]{1,2,0:T(8,128)S(1)} custom-call(f32[1,128,128]{2,1,0:T(8,128)S(1)} %get-tuple-element.29), custom_call_target="InvertDiagBlocksLowerTriangular" | custom-call | tf_op jit(solution)/shard_map/jit(cholesky)/cholesky | solution.py:21
  343.1 11.7 %cholesky.219 = f32[128,128]{1,0:T(8,128)S(1)} custom-call(f32[128,128]{1,0:T(8,128)S(1)} %cholesky.276), custom_call_target="Cholesky" | custom-call | tf_op jit(solution)/shard_map/jit(cholesky)/cholesky | solution.py:21
  354.8 10.2 %custom-call.31 = f32[1,128,128]{1,2,0:T(8,128)S(1)} custom-call(f32[1,128,128]{2,1,0:T(8,128)S(1)} %get-tuple-element.26), custom_call_target="InvertDiagBlocksLowerTriangular" | custom-call | tf_op jit(solution)/shard_map/jit(cholesky)/cholesky | solution.py:21
  366.5 11.7 %cholesky.240 = f32[128,128]{1,0:T(8,128)S(1)} custom-call(f32[128,128]{1,0:T(8,128)S(1)} %cholesky.281), custom_call_target="Cholesky" | custom-call | tf_op jit(solution)/shard_map/jit(cholesky)/cholesky | solution.py:21
  378.2 9.8 %custom-call.32 = f32[1,128,128]{1,2,0:T(8,128)S(1)} custom-call(f32[1,128,128]{2,1,0:T(8,128)S(1)} %get-tuple-element.23), custom_call_target="InvertDiagBlocksLowerTriangular" | custom-call | tf_op jit(solution)/shard_map/jit(cholesky)/cholesky | solution.py:21
  389.9 5.8 cholesky.260
  400.7 9.0 %while.1 = (s32[]{:T(128)}, f32[448,448]{1,0:T(8,128)}, s32[3,2]{0,1:T(2,128)S(1)}, f32[3,128,128]{2,1,0:T(8,128)S(1)}, s32[]{:T(128)}) while((s32[]{:T(128)}, f32[448,448]{1,0:T(8,128)}, s32[3,2]{0,1:T(2,128)S(1)}, f32[3,128,128]{2,1,0:T(8,128)S(1)}, s32[]{:T(128)}) %tuple.46), condition=%wide.while_cond, body=%wide.while_body.sunk | while | flops 2 | bytes 131189 | solution.py:23
  401.6 2.3 bitcast_dynamic-update-slice_fusion.2
  404.5 2.3 bitcast_dynamic-update-slice_fusion.2
  407.5 2.3 bitcast_dynamic-update-slice_fusion.2
  409.8 39.3 %custom-call.33 = f32[4,128,128]{1,2,0:T(8,128)S(1)} custom-call(f32[4,128,128]{2,1,0:T(8,128)S(1)} %pad_maximum_fusion.3), custom_call_target="InvertDiagBlocksLowerTriangular" | custom-call | tf_op jit(solution)/shard_map/triangular_solve | solution.py:23
  454.7 6.2 copy.18
  460.9 6.3 reshape.63
  467.1 28.6 %fusion.60 = f32[448,6400]{1,0:T(8,128)} fusion(bf16[3200,448]{0,1:T(8,128)(2,1)} %reshape.63, bf16[6400,3200]{1,0:T(8,128)(2,1)} %param.3), kind=kOutput, calls=%fused_computation.100 | convolution fusion | flops 18350080000 | bytes 55296000 | tf_op jit(solution)/shard_map/dot_general | solution.py:49
  495.7 28.9 %fusion.61 = f32[448,6400]{1,0:T(8,128)} fusion(bf16[3200,448]{0,1:T(8,128)(2,1)} %reshape.63, bf16[6400,3200]{1,0:T(8,128)(2,1)} %param.4), kind=kOutput, calls=%fused_computation.101 | convolution fusion | flops 18350080000 | bytes 55296000 | tf_op jit(solution)/shard_map/dot_general | solution.py:49
  524.6 9.2 %copy.17 = bf16[8,800,448]{1,0,2:T(8,128)(2,1)} copy(bf16[8,800,448]{1,2,0:T(8,128)(2,1)} %all-gather.5.cloned.1.call-done) | data formatting | bytes 11468800 | tf_op jit(solution)/shard_map/all_gather | solution.py:45
  533.8 11.2 %reshape.61 = bf16[6400,448]{0,1:T(8,128)(2,1)} reshape(bf16[8,800,448]{1,0,2:T(8,128)(2,1)} %copy.17) | data formatting | bytes 11468800
  545.0 8.9 %fusion.55 = f32[448,448]{1,0:T(8,128)S(1)} fusion(bf16[6400,448]{0,1:T(8,128)(2,1)} %reshape.61, f32[448,6400]{1,0:T(8,128)} %fusion.60), kind=kOutput, calls=%fused_computation.97 | convolution fusion | flops 2569011200 | bytes 18006016 | tf_op jit(solution)/shard_map/dot_general | solution.py:11
  553.9 6.7 fusion.11
  560.6 2.5 fusion.48
  563.1 2.7 fusion.47
  565.8 3.1 fusion.53
  569.0 3.1 fusion.8
  572.2 2.5 fusion.46
  574.7 2.7 fusion.49
  577.4 131.7 %all-reduce.9.cloned.1.call-done = (f32[400,400]{1,0:T(8,128)}, f32[400,400]{1,0:T(8,128)}) async-done(((f32[400,400]{1,0:T(8,128)}, f32[400,400]{1,0:T(8,128)}), (f32[400,400]{1,0:T(8,128)}, f32[400,400]{1,0:T(8,128)})) %all-reduce.9.cloned.1.call-update) | async-done | bytes 1280016 | tf_op jit(solution)/shard_map/psum | solution.py:54
  (85 shorter events, 29.8 us)
Async XLA Ops:
  7.2 1.8 copy-start
  7.2 163.3 %reduce-scatter.4.cloned.1.call-start = ((), (), s32[]{:S(2)}) async-start(), calls=%async_computation.4 | async-start | bytes 7372800
  45.8 269.3 %all-reduce.7.cloned.1.call-start = ((), (), s32[]{:S(2)}) async-start(), calls=%async_computation.1 | async-start | bytes 1835008 | tf_op jit(solution)/shard_map/psum | solution.py:42
  172.2 5.1 copy-start.5
  172.2 3.9 collective-permute-start
  176.0 278.6 %all-gather.7.cloned.1.call-start = ((), (), s32[]{:S(2)}) async-start(), calls=%async_computation.3 | async-start | bytes 4014080 | tf_op jit(solution)/shard_map/all_gather | solution.py:44
  176.1 0.9 copy-start.8
  177.0 347.6 %all-gather.5.cloned.1.call-start = ((), (), s32[]{:S(2)}) async-start(), calls=%async_computation.2 | async-start | bytes 7225344 | tf_op jit(solution)/shard_map/all_gather | solution.py:45
  177.6 531.5 %all-reduce.9.cloned.1.call-start = ((), (), s32[]{:S(2)}) async-start(), calls=%async_computation.5 | async-start | bytes 3276800 | tf_op jit(solution)/shard_map/psum | solution.py:54
  318.0 0.9 copy-start.7
  399.8 0.9 copy-start.6
  454.7 108.5 %copy-start.2 = (f32[64,448]{0,1:T(8,128)}, f32[64,448]{0,1:T(8,128)S(1)}, u32[]{:S(2)}) copy-start(f32[64,448]{0,1:T(8,128)S(1)} %fusion.42) | copy-start | bytes 344068
  545.0 8.9 %copy-start.4 = (bf16[6400,448]{0,1:T(8,128)(2,1)S(1)}, bf16[6400,448]{0,1:T(8,128)(2,1)}, u32[]{:S(2)}) copy-start(bf16[6400,448]{0,1:T(8,128)(2,1)} %reshape.61) | copy-start | bytes 17203204
  545.0 20.8 %slice-start = ((s8[11468800]{0:T(1024)(128)(4,1)}), s8[4194304]{0:T(1024)(128)(4,1)S(1)}, s32[]{:S(2)}) async-start(s8[11468800]{0:T(1024)(128)(4,1)} %bitcast.121), calls=%async_computation.6 | async-start | bytes 8388608
  545.0 20.8 %slice-start.1 = ((s8[11468800]{0:T(1024)(128)(4,1)}), s8[4194304]{0:T(1024)(128)(4,1)S(1)}, s32[]{:S(2)}) async-start(s8[11468800]{0:T(1024)(128)(4,1)} %bitcast.121), calls=%async_computation.7 | async-start | bytes 8388608
  553.9 11.9 %slice-start.2 = ((s8[11468800]{0:T(1024)(128)(4,1)}), s8[3080192]{0:T(1024)(128)(4,1)S(1)}, s32[]{:S(2)}) async-start(s8[11468800]{0:T(1024)(128)(4,1)} %bitcast.121), calls=%async_computation.8 | async-start | bytes 6160384
  569.0 3.2 copy-start.3
  569.0 144.3 %copy-start.1 = (bf16[3200,448]{0,1:T(8,128)(2,1)S(1)}, bf16[3200,448]{0,1:T(8,128)(2,1)}, u32[]{:S(2)}) copy-start(bf16[3200,448]{0,1:T(8,128)(2,1)} %param.5) | copy-start | bytes 8601604
Sparse Core Ops, SparseCore 0:
  45.9 124.5 reduce-scatter.3
  176.2 138.9 all-reduce.6
  317.3 27.8 all-gather.6
  347.8 101.0 all-gather.4
  577.5 131.5 all-reduce.8

commit v2 on v1

v2 whole, which is shorter than its diff:
```python
import functools

import jax
import jax.numpy as jnp
from jax import lax
from jax.experimental import pallas as pl
from jax.experimental.pallas import tpu as pltpu
from jax.sharding import PartitionSpec as P

RANK = 400
HIGHEST = lax.Precision.HIGHEST
BLOCK = 128
TILE = 8
VMEM_LIMIT = 58 * 1024 * 1024


def outer(left, right, precision=None):
    return lax.dot_general(
        left, right, (((0,), (0,)), ((), ())), precision=precision, preferred_element_type=jnp.float32
    )


def row_tile(rows):
    for tile in (640, 512, 400, 320, 256, 160, 128, 64, 32, 16):
        if rows % tile == 0:
            return tile
    return rows


def sample_kernel(matrix, sketch, out):
    out[...] = jnp.dot(matrix[...], sketch[...], preferred_element_type=jnp.float32).astype(out.dtype)


def sample(matrix, sketch):
    rows, depth = matrix.shape
    width = sketch.shape[1]
    tile = row_tile(rows)
    return pl.pallas_call(
        sample_kernel,
        grid=(rows // tile,),
        out_shape=jax.ShapeDtypeStruct((rows, width), jnp.bfloat16),
        in_specs=[
            pl.BlockSpec((tile, depth), lambda i: (i, 0)),
            pl.BlockSpec((depth, width), lambda i: (0, 0)),
        ],
        out_specs=pl.BlockSpec((tile, width), lambda i: (i, 0)),
        compiler_params=pltpu.CompilerParams(vmem_limit_bytes=VMEM_LIMIT),
    )(matrix, sketch)


def pair_kernel(matrix, cols, rows, out):
    image = jnp.dot(matrix[...], cols[...], preferred_element_type=jnp.float32)
    upper_part = image.astype(jnp.bfloat16)
    lower_part = (image - upper_part.astype(jnp.float32)).astype(jnp.bfloat16)
    left = rows[...].T
    term = jnp.dot(left, upper_part, preferred_element_type=jnp.float32)
    term += jnp.dot(left, lower_part, preferred_element_type=jnp.float32)

    @pl.when(pl.program_id(0) == 0)
    def _():
        out[...] = term

    @pl.when(pl.program_id(0) > 0)
    def _():
        out[...] += term


def pair_product(matrix, cols, rows):
    height, depth = matrix.shape
    width = cols.shape[1]
    tile = row_tile(height)
    return pl.pallas_call(
        pair_kernel,
        grid=(height // tile,),
        out_shape=jax.ShapeDtypeStruct((width, width), jnp.float32),
        in_specs=[
            pl.BlockSpec((tile, depth), lambda i: (i, 0)),
            pl.BlockSpec((depth, width), lambda i: (0, 0)),
            pl.BlockSpec((tile, width), lambda i: (i, 0)),
        ],
        out_specs=pl.BlockSpec((width, width), lambda i: (0, 0)),
        compiler_params=pltpu.CompilerParams(vmem_limit_bytes=VMEM_LIMIT),
    )(matrix, cols, rows)


def eliminate(block):
    count = block.shape[0] // TILE
    row_ids = lax.broadcasted_iota(jnp.int32, (TILE, BLOCK), 0)
    lane_ids = lax.broadcasted_iota(jnp.int32, (TILE, BLOCK), 1)
    work = [block[t * TILE : (t + 1) * TILE, :] for t in range(count)]
    other = [(lane_ids == row_ids + t * TILE).astype(jnp.float32) for t in range(count)]
    for step in range(count * TILE):
        home, place = divmod(step, TILE)
        column = [jnp.broadcast_to(work[t][:, step : step + 1], (TILE, BLOCK)) for t in range(home, count)]
        scale = 1.0 / column[0][place : place + 1, :]
        pivot_row = work[home][place : place + 1, :] * scale
        other_row = other[home][place : place + 1, :] * scale
        for t in range(home, count):
            factor = column[t - home]
            if t == home:
                factor = jnp.where(row_ids > place, factor, 0.0)
            work[t] = work[t] - factor * pivot_row
            other[t] = other[t] - factor * other_row
    done = []
    for t in range(count):
        diagonal = jnp.sum(jnp.where(lane_ids == row_ids + t * TILE, work[t], 0.0), axis=1, keepdims=True)
        done.append(other[t] / jnp.sqrt(diagonal))
    return jnp.concatenate(done, axis=0)


def factor_kernel(gram, out, held):
    size = gram.shape[0]
    padded = held.shape[0]
    ids_r = lax.broadcasted_iota(jnp.int32, (padded, padded), 0)
    ids_c = lax.broadcasted_iota(jnp.int32, (padded, padded), 1)
    unit = (ids_r == ids_c).astype(jnp.float32)
    held[:, :padded] = unit
    held[:, padded:] = unit
    held[:size, :size] = gram[...]
    blocks = padded // BLOCK

    def one(k, carry):
        at = pl.multiple_of(k * BLOCK, BLOCK)
        inverse = eliminate(held[pl.ds(at, BLOCK), pl.ds(at, BLOCK)])
        strip = jnp.dot(inverse, held[pl.ds(at, BLOCK), :], precision=HIGHEST, preferred_element_type=jnp.float32)
        held[pl.ds(at, BLOCK), :] = strip

        def trail(i, inner):
            low = pl.multiple_of(i * BLOCK, BLOCK)
            side = held[pl.ds(at, BLOCK), pl.ds(low, BLOCK)]
            held[pl.ds(low, BLOCK), :] -= jnp.dot(
                side.T, held[pl.ds(at, BLOCK), :], precision=HIGHEST, preferred_element_type=jnp.float32
            )
            return inner

        lax.fori_loop(k + 1, blocks, trail, 0)
        return carry

    lax.fori_loop(0, blocks, one, 0)
    out[...] = held[:size, padded : padded + size]


def inverse_factor(gram):
    size = gram.shape[0]
    padded = -(-size // BLOCK) * BLOCK
    whole = pl.pallas_call(
        factor_kernel,
        out_shape=jax.ShapeDtypeStruct((size, size), jnp.float32),
        in_specs=[pl.BlockSpec(memory_space=pltpu.VMEM)],
        out_specs=pl.BlockSpec(memory_space=pltpu.VMEM),
        scratch_shapes=[pltpu.VMEM((padded, 2 * padded), jnp.float32)],
    )(gram)
    return whole[size - RANK :]


def reduce_kernel(n_row, n_col, x, out, row_land, col_land, part, total, *sems):
    send_a, recv_a, send_b, recv_b, send_c, recv_c, send_d, recv_d = sems
    me_row, me_col = lax.axis_index("row"), lax.axis_index("col")
    big = x.shape[0] // n_row
    small = big // n_col

    def peer(me, shift, count):
        return lax.rem(me + shift, count)

    def row_of(shift):
        return (peer(me_row, shift, n_row), me_col)

    def col_of(shift):
        return (me_row, peer(me_col, shift, n_col))

    def copy(source, target, send, recv, device):
        return pltpu.make_async_remote_copy(
            src_ref=source, dst_ref=target, send_sem=send, recv_sem=recv,
            device_id=device, device_id_type=pl.DeviceIdType.MESH,
        )

    def at(index, size):
        return pl.ds(pl.multiple_of(index * size, TILE), size)

    barrier = pltpu.get_barrier_semaphore()
    for d in range(1, n_row):
        pl.semaphore_signal(barrier, inc=1, device_id=row_of(d), device_id_type=pl.DeviceIdType.MESH)
    for d in range(1, n_col):
        pl.semaphore_signal(barrier, inc=1, device_id=col_of(d), device_id_type=pl.DeviceIdType.MESH)
    pl.semaphore_wait(barrier, n_row + n_col - 2)

    first = []
    for d in range(1, n_row):
        chunk = x.at[at(peer(me_row, d, n_row), big), :]
        first.append(copy(chunk, row_land.at[d - 1], send_a.at[d - 1], recv_a.at[d - 1], row_of(d)))
        first[-1].start()
    summed = x[at(me_row, big), :]
    for d in range(1, n_row):
        first[d - 1].wait_recv()
        summed += row_land[d - 1]
    part[...] = summed

    second = []
    for d in range(1, n_col):
        chunk = part.at[at(peer(me_col, d, n_col), small), :]
        second.append(copy(chunk, col_land.at[d - 1], send_b.at[d - 1], recv_b.at[d - 1], col_of(d)))
        second[-1].start()
    summed = part[at(me_col, small), :]
    for d in range(1, n_col):
        second[d - 1].wait_recv()
        summed += col_land[d - 1]
    total[...] = summed

    mine = pl.ds(pl.multiple_of(me_row * big + me_col * small, TILE), small)
    third = []
    for d in range(1, n_col):
        third.append(copy(total, out.at[mine, :], send_c.at[d - 1], recv_c.at[d - 1], col_of(d)))
        third[-1].start()
    out[mine, :] = summed
    for d in range(1, n_col):
        third[d - 1].wait_recv()

    fourth = []
    for d in range(1, n_row):
        chunk = out.at[at(me_row, big), :]
        fourth.append(copy(chunk, chunk, send_d.at[d - 1], recv_d.at[d - 1], row_of(d)))
        fourth[-1].start()
    for d in range(1, n_row):
        fourth[d - 1].wait_recv()
    for sent in first + second + third + fourth:
        sent.wait_send()


def reduce_all(value, collective_id):
    n_row, n_col = lax.axis_size("row"), lax.axis_size("col")
    height, width = value.shape
    grain = n_row * n_col * TILE
    padded = -(-height // grain) * grain
    value = jnp.pad(value, ((0, padded - height), (0, 0)))
    big = padded // n_row
    small = big // n_col
    dma = pltpu.SemaphoreType.DMA
    result = pl.pallas_call(
        functools.partial(reduce_kernel, n_row, n_col),
        out_shape=jax.ShapeDtypeStruct((padded, width), jnp.float32),
        in_specs=[pl.BlockSpec(memory_space=pltpu.VMEM)],
        out_specs=pl.BlockSpec(memory_space=pltpu.VMEM),
        scratch_shapes=[
            pltpu.VMEM((n_row - 1, big, width), jnp.float32),
            pltpu.VMEM((n_col - 1, small, width), jnp.float32),
            pltpu.VMEM((big, width), jnp.float32),
            pltpu.VMEM((small, width), jnp.float32),
        ]
        + [dma((n_row - 1,)), dma((n_row - 1,)), dma((n_col - 1,)), dma((n_col - 1,))]
        + [dma((n_col - 1,)), dma((n_col - 1,)), dma((n_row - 1,)), dma((n_row - 1,))],
        compiler_params=pltpu.CompilerParams(collective_id=collective_id, has_side_effects=True),
    )(value)
    return result[:height]


def column_route(n_row, n_col):
    ratio = n_col // n_row
    route = []
    for source in range(n_row):
        for shard in range(n_col):
            half, target = divmod(shard, n_row)
            route.append((source * n_col + shard, target * n_col + source * ratio + half))
    return route


def body(corner, edge, sketch):
    n_row, n_col = lax.axis_size("row"), lax.axis_size("col")
    both = ("row", "col")
    shard = lax.psum_scatter(sample(corner, sketch), "col", scatter_dimension=0, tiled=True)
    moved = lax.ppermute(shard, both, column_route(n_row, n_col))
    cols = lax.all_gather(moved, "row", axis=0, tiled=True)
    rows = lax.all_gather(shard, "col", axis=0, tiled=True)
    gram = reduce_all(outer(shard, shard), 0)
    inverse = inverse_factor(gram)

    def renormalize(matrix):
        total = pair_product(matrix, cols, rows)
        half = jnp.dot(inverse, total, precision=HIGHEST)
        return lax.dot_general(half, inverse, (((1,), (1,)), ((), ())), precision=HIGHEST)

    stacked = jnp.concatenate([renormalize(corner), renormalize(edge)], axis=0)
    result = reduce_all(stacked, 1)
    return result[:RANK], result[RANK:]


def solution(mesh):
    placed = (P("row", "col"), P("row", "col"), P("col", None))
    return jax.shard_map(body, mesh=mesh, in_specs=placed, out_specs=(P(), P()), check_vma=False)
```

time: 726 us -> 518 us (0.71)
  Pallas kernels: 0 us -> 292 us
  waiting for transfers between devices: 394 us -> 160 us
  matrix products: 131 us -> 8.94 us
  other arithmetic: 114 us -> 1.56 us
  local copies, waits for them, and re-layouts: 62.8 us -> 32.2 us
    pallas_call x0 -> x6, Pallas kernels: none -> 292 us  [the longest x2 138 us: reduce_all(): pl.pallas_call(functools.partial(reduce_kernel, n_row, n_col), out_shape=...]
    psum x2 -> x0, waiting for transfers between devices: 269 us -> none  [the longest x1 137 us: body(): gram = lax.psum(outer(shard, shard), both)]
    unnamed x6 -> x3, waiting for transfers between devices: 125 us -> 0.05 us
    reduce_scatter x0 -> x1, waiting for transfers between devices: none -> 125 us  [body(): lax.psum_scatter(sample(corner, sketch), 'col', scatter_dimension=0, tile...]
    another operation x21 -> x0, other arithmetic: 112 us -> none  [the longest x14 72.9 us: inverse_factor(): lower = jnp.linalg.cholesky(gram)]
    dot_general x8 -> x1, matrix products: 110 us -> 0.66 us  [outer(): lax.dot_general(left, right, (((0,), (0,)), ((), ())), precision=precisio...]
    all_gather x1, waiting for transfers between devices: 0.01 us -> 34.8 us  [body(): rows = lax.all_gather(shard, 'col', axis=0, tiled=True)]
    unnamed x30 -> x8, local copies, waits for them, and re-layouts: 37.1 us -> 7.57 us
  transfers between devices with their start and end apart: 6 -> 4, of which waited for: 3 -> 2; matrix products, arithmetic and copies ran while one was open for 29% -> 2% of each run, Pallas kernels for 0% -> 26%
where the time goes in v2:
time: 518 us; the launch traced here: 509 us
  Pallas kernels  292 us (56%)
  waiting for transfers between devices  160 us (31%)
  local copies, waits for them, and re-layouts  32.2 us (6%)
  between operations  13.8 us (3%)
  matrix products  8.94 us (2%)
    pallas_call x2, Pallas kernels, reduce_all(): pl.pallas_call(functools.partial(reduce_kernel, n_row, n_col), out_shape=...  138 us
    reduce_scatter x1, waiting for transfers between devices, body(): lax.psum_scatter(sample(corner, sketch), 'col', scatter_dimension=0, tile...  125 us
    pallas_call x2, Pallas kernels, pair_product(): pl.pallas_call(pair_kernel, grid=(height // tile,), out_shape=jax.ShapeDt...  75.3 us
    pallas_call x1, Pallas kernels, inverse_factor(): pl.pallas_call(factor_kernel, out_shape=jax.ShapeDtypeStruct((size, size)...  51.4 us
    all_gather x1, waiting for transfers between devices, body(): rows = lax.all_gather(shard, 'col', axis=0, tiled=True)  34.8 us
    pallas_call x1, Pallas kernels, sample(): pl.pallas_call(sample_kernel, grid=(rows // tile,), out_shape=jax.ShapeDt...  27.8 us
    all_gather x1, local copies, waits for them, and re-layouts, body(): rows = lax.all_gather(shard, 'col', axis=0, tiled=True)  11 us
  transfers between devices with their start and end apart: 4, of which 2 were waited for; matrix products, arithmetic and copies ran while one was open for 2% of the time, Pallas kernels for 26%

profile of v2, /device:TPU:0, one launch (start us, length us, event | category | flops | bytes accessed | tf_op | source)
XLA Modules:
  0.0 508.9 jit_solution(17477989053510521934)
XLA Ops:
  7.2 0.0 reduce-scatter.2.cloned.1.call-start
  7.2 5.5 %copy.9.sketch = bf16[3200,448]{1,0:T(8,128)(2,1)} copy(bf16[3200,448]{0,1:T(8,128)(2,1)} %param.5) | data formatting | bytes 5734400 | tf_op args[2]
  12.7 27.8 %shard_map.50 = bf16[6400,448]{1,0:T(8,128)(2,1)} custom-call(bf16[6400,3200]{1,0:T(8,128)(2,1)} %matrix.4, bf16[3200,448]{1,0:T(8,128)(2,1)} %copy.9.sketch), custom_call_target="tpu_custom_call" | custom-call | tf_op jit(solution)/shard_map/pallas_call | solution.py:38
  40.5 0.0 reduce-scatter.2.cloned.1.call-update
  40.5 0.0 all-gather.5.cloned.1.call-start
  40.6 124.6 %reduce-scatter.2.cloned.1.call-done = bf16[800,448]{1,0:T(8,128)(2,1)} async-done(((bf16[6400,448]{1,0:T(8,128)(2,1)}), bf16[800,448]{1,0:T(8,128)(2,1)}) %reduce-scatter.2.cloned.1.call-update) | async-done | bytes 716816 | tf_op jit(solution)/shard_map/reduce_scatter | solution.py:269
  165.2 1.8 copy.11
  167.0 0.7 collective-permute-start
  167.7 0.0 collective-permute-done
  167.7 0.0 copy-start.2
  167.7 0.9 copy-done.2
  168.6 0.0 all-gather.5.cloned.1.call-update
  168.6 0.0 all-gather.7.cloned.1.call-start
  168.7 1.2 copy.13
  169.9 0.0 all-gather.7.cloned.1.call-update
  169.9 0.7 fusion.9
  170.6 1.1 pad.8.x
  171.7 82.6 %shard_map.51 = f32[512,448]{1,0:T(8,128)} custom-call(f32[512,448]{1,0:T(8,128)} %pad.8.x), custom_call_target="tpu_custom_call" | custom-call | tf_op jit(solution)/shard_map/pallas_call | solution.py:238
  254.4 2.2 slice.15.gram
  256.6 51.4 %shard_map.52 = f32[448,448]{1,0:T(8,128)} custom-call(f32[448,448]{1,0:T(8,128)} %slice.15.gram), custom_call_target="tpu_custom_call" | custom-call | tf_op jit(solution)/shard_map/pallas_call | solution.py:146
  308.0 5.8 %copy.12 = bf16[4,800,448]{2,1,0:T(8,128)(2,1)} copy(bf16[4,800,448]{1,2,0:T(8,128)(2,1)} %all-gather.5.cloned.1.call-done) | data formatting | bytes 5734400 | tf_op jit(solution)/shard_map/all_gather | solution.py:271
  313.8 34.8 %all-gather.7.cloned.1.call-done = bf16[8,800,448]{1,2,0:T(8,128)(2,1)} async-done(((bf16[1,800,448]{1,2,0:T(8,128)(2,1)}), bf16[8,800,448]{1,2,0:T(8,128)(2,1)}) %all-gather.7.cloned.1.call-update) | async-done | bytes 5734416 | tf_op jit(solution)/shard_map/all_gather | solution.py:272
  348.6 11.0 %copy.14 = bf16[8,800,448]{2,1,0:T(8,128)(2,1)} copy(bf16[8,800,448]{1,2,0:T(8,128)(2,1)} %all-gather.7.cloned.1.call-done) | data formatting | bytes 11468800 | tf_op jit(solution)/shard_map/all_gather | solution.py:272
  359.7 37.6 %shard_map.53 = f32[448,448]{1,0:T(8,128)} custom-call(bf16[6400,3200]{1,0:T(8,128)(2,1)} %matrix.4, bf16[3200,448]{1,0:T(8,128)(2,1)} %bitcast.12, bf16[6400,448]{1,0:T(8,128)(2,1)} %bitcast.10), custom_call_target="tpu_custom_call" | custom-call | tf_op jit(solution)/shard_map/pallas_call | solution.py:72
  397.3 2.7 fusion.6
  399.9 1.5 fusion.4
  401.4 37.7 %shard_map.54 = f32[448,448]{1,0:T(8,128)} custom-call(bf16[6400,3200]{1,0:T(8,128)(2,1)} %matrix.5, bf16[3200,448]{1,0:T(8,128)(2,1)} %bitcast.13, bf16[6400,448]{1,0:T(8,128)(2,1)} %bitcast.11), custom_call_target="tpu_custom_call" | custom-call | tf_op jit(solution)/shard_map/pallas_call | solution.py:72
  439.1 2.7 fusion.2
  441.8 1.5 fusion
  443.3 1.6 select_maximum_fusion.x
  444.8 54.9 %shard_map.55 = f32[1024,400]{1,0:T(8,128)} custom-call(f32[1024,400]{1,0:T(8,128)} %select_maximum_fusion.x), custom_call_target="tpu_custom_call" | custom-call | tf_op jit(solution)/shard_map/pallas_call | solution.py:238
  499.7 2.7 fusion.8
  (5 shorter events, 0.0 us)
Async XLA Ops:
  7.2 158.0 %reduce-scatter.2.cloned.1.call-start = ((), (), s32[]{:S(2)}) async-start(), calls=%async_computation.1 | async-start | bytes 7372800 | tf_op jit(solution)/shard_map/reduce_scatter | solution.py:269
  40.5 267.5 %all-gather.5.cloned.1.call-start = ((), (), s32[]{:S(2)}) async-start(), calls=%async_computation.2 | async-start | bytes 4014080 | tf_op jit(solution)/shard_map/all_gather | solution.py:271
  165.2 3.5 copy-start.1
  167.0 0.7 collective-permute-start
  167.7 0.9 copy-start.2
  168.6 180.0 %all-gather.7.cloned.1.call-start = ((), (), s32[]{:S(2)}) async-start(), calls=%async_computation.3 | async-start | bytes 7225344 | tf_op jit(solution)/shard_map/all_gather | solution.py:272
  359.7 37.6 %copy-start = (f32[448,448]{1,0:T(8,128)S(1)}, f32[448,448]{1,0:T(8,128)}, u32[]{:S(2)}) copy-start(f32[448,448]{1,0:T(8,128)} %shard_map.52) | copy-start | bytes 2408452
Sparse Core Ops, SparseCore 0:
  40.6 124.5 reduce-scatter.1
  168.7 78.5 all-gather.4
  250.1 98.4 all-gather.6

commit v3 on v2

--- a/solution.py
+++ b/solution.py
@@ -48,39 +48,62 @@
     )(matrix, sketch)
 
 
-def pair_kernel(matrix, cols, rows, out):
-    image = jnp.dot(matrix[...], cols[...], preferred_element_type=jnp.float32)
-    upper_part = image.astype(jnp.bfloat16)
-    lower_part = (image - upper_part.astype(jnp.float32)).astype(jnp.bfloat16)
-    left = rows[...].T
-    term = jnp.dot(left, upper_part, preferred_element_type=jnp.float32)
-    term += jnp.dot(left, lower_part, preferred_element_type=jnp.float32)
-
-    @pl.when(pl.program_id(0) == 0)
-    def _():
-        out[...] = term
-
-    @pl.when(pl.program_id(0) > 0)
-    def _():
-        out[...] += term
-
-
-def pair_product(matrix, cols, rows):
+def image_kernel(matrix, cols, out):
+    out[...] = jnp.dot(matrix[...], cols[...], preferred_element_type=jnp.float32)
+
+
+def image_of(matrix, cols):
     height, depth = matrix.shape
     width = cols.shape[1]
     tile = row_tile(height)
     return pl.pallas_call(
-        pair_kernel,
+        image_kernel,
         grid=(height // tile,),
-        out_shape=jax.ShapeDtypeStruct((width, width), jnp.float32),
+        out_shape=jax.ShapeDtypeStruct((height, width), jnp.float32),
         in_specs=[
             pl.BlockSpec((tile, depth), lambda i: (i, 0)),
             pl.BlockSpec((depth, width), lambda i: (0, 0)),
-            pl.BlockSpec((tile, width), lambda i: (i, 0)),
         ],
-        out_specs=pl.BlockSpec((width, width), lambda i: (0, 0)),
+        out_specs=pl.BlockSpec((tile, width), lambda i: (i, 0)),
+        cost_estimate=pl.CostEstimate(
+            flops=2 * height * depth * width, bytes_accessed=2 * height * depth, transcendentals=0
+        ),
         compiler_params=pltpu.CompilerParams(vmem_limit_bytes=VMEM_LIMIT),
-    )(matrix, cols, rows)
+    )(matrix, cols)
+
+
+def left_kernel(rows, first, second, first_out, second_out):
+    left = rows[...].T
+
+    def term(image):
+        upper_part = image.astype(jnp.bfloat16)
+        lower_part = (image - upper_part.astype(jnp.float32)).astype(jnp.bfloat16)
+        found = jnp.dot(left, upper_part, preferred_element_type=jnp.float32)
+        return found + jnp.dot(left, lower_part, preferred_element_type=jnp.float32)
+
+    @pl.when(pl.program_id(0) == 0)
+    def _():
+        first_out[...] = jnp.zeros_like(first_out)
+        second_out[...] = jnp.zeros_like(second_out)
+
+    first_out[...] += term(first[...])
+    second_out[...] += term(second[...])
+
+
+def left_products(rows, first, second):
+    height, width = rows.shape
+    tile = row_tile(height)
+    tall = pl.BlockSpec((tile, width), lambda i: (i, 0))
+    square = pl.BlockSpec((width, width), lambda i: (0, 0))
+    shape = jax.ShapeDtypeStruct((width, width), jnp.float32)
+    return pl.pallas_call(
+        left_kernel,
+        grid=(height // tile,),
+        out_shape=(shape, shape),
+        in_specs=[tall, tall, tall],
+        out_specs=(square, square),
+        compiler_params=pltpu.CompilerParams(vmem_limit_bytes=VMEM_LIMIT),
+    )(rows, first, second)
 
 
 def eliminate(block):
@@ -149,6 +172,9 @@
         in_specs=[pl.BlockSpec(memory_space=pltpu.VMEM)],
         out_specs=pl.BlockSpec(memory_space=pltpu.VMEM),
         scratch_shapes=[pltpu.VMEM((padded, 2 * padded), jnp.float32)],
+        cost_estimate=pl.CostEstimate(
+            flops=100 * padded * padded * padded, bytes_accessed=8 * size * size, transcendentals=0
+        ),
     )(gram)
     return whole[size - RANK :]
 
@@ -267,18 +293,20 @@
     n_row, n_col = lax.axis_size("row"), lax.axis_size("col")
     both = ("row", "col")
     shard = lax.psum_scatter(sample(corner, sketch), "col", scatter_dimension=0, tiled=True)
+    gram = reduce_all(outer(shard, shard), 0)
+    shard, gram = lax.optimization_barrier((shard, gram))
     moved = lax.ppermute(shard, both, column_route(n_row, n_col))
     cols = lax.all_gather(moved, "row", axis=0, tiled=True)
     rows = lax.all_gather(shard, "col", axis=0, tiled=True)
-    gram = reduce_all(outer(shard, shard), 0)
     inverse = inverse_factor(gram)
-
-    def renormalize(matrix):
-        total = pair_product(matrix, cols, rows)
+    corner_image, edge_image = image_of(corner, cols), image_of(edge, cols)
+
+    def renormalize(total):
         half = jnp.dot(inverse, total, precision=HIGHEST)
         return lax.dot_general(half, inverse, (((1,), (1,)), ((), ())), precision=HIGHEST)
 
-    stacked = jnp.concatenate([renormalize(corner), renormalize(edge)], axis=0)
+    corner_sum, edge_sum = left_products(rows, corner_image, edge_image)
+    stacked = jnp.concatenate([renormalize(corner_sum), renormalize(edge_sum)], axis=0)
     result = reduce_all(stacked, 1)
     return result[:RANK], result[RANK:]
 

time: 518 us -> 497 us (0.959)
  Pallas kernels: 292 us -> 250 us
  waiting for transfers between devices: 160 us -> 180 us
    pallas_call x2, Pallas kernels: 138 us -> 89.6 us  [reduce_all(): pl.pallas_call(functools.partial(reduce_kernel, n_row, n_col), out_shape=...]
    all_gather x1, waiting for transfers between devices: 0.01 us -> 17.3 us  [body(): cols = lax.all_gather(moved, 'row', axis=0, tiled=True)]
    pallas_call x2 -> x3, Pallas kernels: 75.3 us -> 80.7 us  [the longest x2 58.8 us: image_of(): pl.pallas_call(image_kernel, grid=(height // tile,), out_shape=jax.ShapeD...]
  transfers between devices with their start and end apart: 4 -> 4, of which waited for: 2 -> 3; matrix products, arithmetic and copies ran while one was open for 2% -> 1% of each run, Pallas kernels for 26% -> 23%
where the time goes in v3:
time: 497 us; the launch traced here: 487 us
  Pallas kernels  250 us (50%)
  waiting for transfers between devices  180 us (36%)
  local copies, waits for them, and re-layouts  31.2 us (6%)
  between operations  13.9 us (3%)
  matrix products  9.27 us (2%)
    reduce_scatter x1, waiting for transfers between devices, body(): lax.psum_scatter(sample(corner, sketch), 'col', scatter_dimension=0, tile...  125 us
    pallas_call x2, Pallas kernels, reduce_all(): pl.pallas_call(functools.partial(reduce_kernel, n_row, n_col), out_shape=...  89.6 us
    pallas_call x2, Pallas kernels, image_of(): pl.pallas_call(image_kernel, grid=(height // tile,), out_shape=jax.ShapeD...  58.8 us
    pallas_call x1, Pallas kernels, inverse_factor(): pl.pallas_call(factor_kernel, out_shape=jax.ShapeDtypeStruct((size, size)...  51.4 us
    all_gather x1, waiting for transfers between devices, body(): rows = lax.all_gather(shard, 'col', axis=0, tiled=True)  38.5 us
    pallas_call x1, Pallas kernels, sample(): pl.pallas_call(sample_kernel, grid=(rows // tile,), out_shape=jax.ShapeDt...  27.8 us
    pallas_call x1, Pallas kernels, left_products(): pl.pallas_call(left_kernel, grid=(height // tile,), out_shape=(shape, sha...  21.9 us
    all_gather x1, waiting for transfers between devices, body(): cols = lax.all_gather(moved, 'row', axis=0, tiled=True)  17.3 us
  transfers between devices with their start and end apart: 4, of which 3 were waited for; matrix products, arithmetic and copies ran while one was open for 1% of the time, Pallas kernels for 23%

profile of v3, /device:TPU:0, one launch (start us, length us, event | category | flops | bytes accessed | tf_op | source)
XLA Modules:
  0.0 486.9 jit_solution(5855081475643301872)
XLA Ops:
  7.2 0.0 reduce-scatter.2.cloned.1.call-start
  7.2 5.4 %copy.9.sketch = bf16[3200,448]{1,0:T(8,128)(2,1)} copy(bf16[3200,448]{0,1:T(8,128)(2,1)} %param.5) | data formatting | bytes 5734400 | tf_op args[2]
  12.7 27.8 %shard_map.50 = bf16[6400,448]{1,0:T(8,128)(2,1)} custom-call(bf16[6400,3200]{1,0:T(8,128)(2,1)} %matrix.4, bf16[3200,448]{1,0:T(8,128)(2,1)} %copy.9.sketch), custom_call_target="tpu_custom_call" | custom-call | tf_op jit(solution)/shard_map/pallas_call | solution.py:38
  40.5 0.0 reduce-scatter.2.cloned.1.call-update
  40.5 0.0 all-gather.7.cloned.1.call-start
  40.6 124.6 %reduce-scatter.2.cloned.1.call-done = bf16[800,448]{1,0:T(8,128)(2,1)} async-done(((bf16[6400,448]{1,0:T(8,128)(2,1)}), bf16[800,448]{1,0:T(8,128)(2,1)}) %reduce-scatter.2.cloned.1.call-update) | async-done | bytes 716816 | tf_op jit(solution)/shard_map/reduce_scatter | solution.py:295
  165.2 2.1 fusion.9
  167.3 1.1 pad.8.x
  168.4 34.8 %shard_map.51 = f32[512,448]{1,0:T(8,128)} custom-call(f32[512,448]{1,0:T(8,128)} %pad.8.x), custom_call_target="tpu_custom_call" | custom-call | tf_op jit(solution)/shard_map/pallas_call | solution.py:264
  203.2 2.2 slice.15.gram
  205.4 0.8 copy.13
  206.2 0.7 collective-permute-start
  207.0 0.9 copy-done.3
  207.9 0.0 all-gather.7.cloned.1.call-update
  207.9 0.2 all-gather.5.cloned.1.call-start
  208.1 1.2 copy.11
  209.3 0.0 all-gather.5.cloned.1.call-update
  209.4 51.4 %shard_map.52 = f32[448,448]{1,0:T(8,128)} custom-call(f32[448,448]{1,0:T(8,128)} %slice.15.gram), custom_call_target="tpu_custom_call" | custom-call | flops 13421772800 | bytes 1605632 | tf_op jit(solution)/shard_map/pallas_call | solution.py:169
  260.8 17.3 %all-gather.7.cloned.1.call-done = bf16[4,800,448]{1,2,0:T(8,128)(2,1)} async-done(((bf16[1,800,448]{1,2,0:T(8,128)(2,1)}), bf16[4,800,448]{1,2,0:T(8,128)(2,1)}) %all-gather.7.cloned.1.call-update) | async-done | bytes 2867216 | tf_op jit(solution)/shard_map/all_gather | solution.py:299
  278.0 5.8 %copy.14 = bf16[4,800,448]{2,1,0:T(8,128)(2,1)} copy(bf16[4,800,448]{1,2,0:T(8,128)(2,1)} %all-gather.7.cloned.1.call-done) | data formatting | bytes 5734400 | tf_op jit(solution)/shard_map/all_gather | solution.py:299
  283.8 29.4 %shard_map.53.first = f32[6400,448]{1,0:T(8,128)} custom-call(bf16[6400,3200]{1,0:T(8,128)(2,1)} %matrix.4, bf16[3200,448]{1,0:T(8,128)(2,1)} %bitcast.11), custom_call_target="tpu_custom_call" | custom-call | flops 18350080000 | bytes 40960000 | tf_op jit(solution)/shard_map/pallas_call | solution.py:59
  313.2 29.5 %shard_map.54.second = f32[6400,448]{1,0:T(8,128)} custom-call(bf16[6400,3200]{1,0:T(8,128)(2,1)} %matrix.5, bf16[3200,448]{1,0:T(8,128)(2,1)} %bitcast.12), custom_call_target="tpu_custom_call" | custom-call | flops 18350080000 | bytes 40960000 | tf_op jit(solution)/shard_map/pallas_call | solution.py:59
  342.7 38.5 %all-gather.5.cloned.1.call-done = bf16[8,800,448]{1,2,0:T(8,128)(2,1)} async-done(((bf16[1,800,448]{1,2,0:T(8,128)(2,1)}), bf16[8,800,448]{1,2,0:T(8,128)(2,1)}) %all-gather.5.cloned.1.call-update) | async-done | bytes 5734416 | tf_op jit(solution)/shard_map/all_gather | solution.py:300
  381.2 11.0 %copy.12 = bf16[8,800,448]{2,1,0:T(8,128)(2,1)} copy(bf16[8,800,448]{1,2,0:T(8,128)(2,1)} %all-gather.5.cloned.1.call-done) | data formatting | bytes 11468800 | tf_op jit(solution)/shard_map/all_gather | solution.py:300
  392.2 21.9 %shard_map.55 = (f32[448,448]{1,0:T(8,128)}, f32[448,448]{1,0:T(8,128)}) custom-call(bf16[6400,448]{1,0:T(8,128)(2,1)} %bitcast.10, f32[6400,448]{1,0:T(8,128)} %shard_map.53.first, f32[6400,448]{1,0:T(8,128)} %shard_map.54.second), custom_call_target="tpu_custom_call" | custom-call | tf_op jit(solution)/shard_map/pallas_call | solution.py:99
  414.1 2.7 fusion.6
  416.8 1.5 fusion.4
  418.3 1.5 fusion.2
  419.8 1.5 fusion
  421.3 1.6 select_maximum_fusion.x
  422.9 54.8 %shard_map.56 = f32[1024,400]{1,0:T(8,128)} custom-call(f32[1024,400]{1,0:T(8,128)} %select_maximum_fusion.x), custom_call_target="tpu_custom_call" | custom-call | tf_op jit(solution)/shard_map/pallas_call | solution.py:264
  477.7 2.7 fusion.8
  (8 shorter events, 0.0 us)
Async XLA Ops:
  7.2 158.0 %reduce-scatter.2.cloned.1.call-start = ((), (), s32[]{:S(2)}) async-start(), calls=%async_computation.1 | async-start | bytes 7372800 | tf_op jit(solution)/shard_map/reduce_scatter | solution.py:295
  40.5 237.5 %all-gather.7.cloned.1.call-start = ((), (), s32[]{:S(2)}) async-start(), calls=%async_computation.3 | async-start | bytes 4014080 | tf_op jit(solution)/shard_map/all_gather | solution.py:299
  167.3 38.2 %copy-start.1 = (bf16[800,448]{1,0:T(8,128)(2,1)S(1)}, bf16[800,448]{1,0:T(8,128)(2,1)}, u32[]{:S(2)}) copy-start(bf16[800,448]{1,0:T(8,128)(2,1)} %reduce-scatter.2.cloned.1.call-done) | copy-start | bytes 2150404
  206.2 0.7 collective-permute-start
  207.0 0.9 copy-start.3
  207.9 173.3 %all-gather.5.cloned.1.call-start = ((), (), s32[]{:S(2)}) async-start(), calls=%async_computation.2 | async-start | bytes 7225344 | tf_op jit(solution)/shard_map/all_gather | solution.py:300
  392.2 21.9 %copy-start = (f32[448,448]{1,0:T(8,128)S(1)}, f32[448,448]{1,0:T(8,128)}, u32[]{:S(2)}) copy-start(f32[448,448]{1,0:T(8,128)} %shard_map.52) | copy-start | bytes 2408452
  414.1 4.2 copy-start.2
Sparse Core Ops, SparseCore 0:
  40.6 124.5 reduce-scatter.1
  208.0 69.9 all-gather.6
  280.8 100.3 all-gather.4
